TPU v7x, 32 devices: a whole 2x2x4 slice. The times are simulated.
32 devices in a mesh: seq: 16 (over z, y, core), mp: 2 (over x).
Axes of the slice: x: 2, y: 2, z: 4, core: 2. Of those that a mesh axis runs over, the one named last changes fastest.
Arguments:
- shared_qk: bfloat16 [2048, 4096], P('seq', 'mp'), may hold values from -40 to 40
- values: bfloat16 [2048, 4096], P('seq', 'mp'), may hold values from -6 to 6
- buckets: int32 [2048, 32], P('seq', 'mp'), may hold values from 0 to 15, as said below
- counts: int32 [16, 32, 16], P(None, 'mp'), may hold values from 0 to 16, as said below
- w_out: bfloat16 [4096, 4096], P('mp'), may hold values from -0.09375 to 0.09375
Outputs:
- projected: bfloat16 [2048, 4096], P('seq', 'mp')
Inputs may be any that keep to these rules, and one draw needn't show every extreme that they name: `buckets`: in each head at most 16 tokens among rows d * 128 to (d + 1) * 128 - 1 name one bucket, and in each head one bucket is named by exactly 16 tokens of every such group of rows. counts[d, h, b] is the number of rows among d * 128 to (d + 1) * 128 - 1 whose bucket in head h is b.
All inputs are finite; a program needn't handle non-finite values.
Results may differ from a plain program's by a relative error of at most 0.0057.
Values may be sent and summed in bfloat16 or wider, within the bound.
No kernel may reach another device: no remote copies, remote signals or barrier semaphores. Data moves between devices by JAX's collectives and lax.ppermute only.
A program may use at most 64 MiB of HBM per device.

v0:
```python
import math
import jax
import jax.numpy as jnp
from jax import lax
from jax.sharding import PartitionSpec as P

BLOCK = 256
SELF_SCORE = -100000.0


def passed_along(shard, axis, by):
    devices = lax.axis_size(axis)
    return lax.ppermute(shard, axis, [(i, (i + by) % devices) for i in range(devices)])


def block_attention(queries, window, window_live):
    head_dim = queries.shape[-1]
    block_rows = queries.shape[-2]
    key_rows = window[..., :head_dim]
    value_rows = window[..., head_dim:]
    scores = jnp.einsum("cqd,ckd->cqk", queries, key_rows, preferred_element_type=jnp.float32) * (
        1.0 / math.sqrt(head_dim)
    )
    query_place = jnp.arange(block_rows)[:, None] + block_rows
    key_place = jnp.arange(2 * block_rows)[None, :]
    itself = query_place == key_place
    scores = jnp.where(itself[None], SELF_SCORE, scores)
    allowed = window_live[:, None, :] | itself[None]
    row_max = jnp.max(jnp.where(allowed, scores, -1e30), axis=-1, keepdims=True)
    exp_terms = jnp.where(allowed, jnp.exp(scores - row_max), 0.0)
    weights = (exp_terms / jnp.sum(exp_terms, axis=-1, keepdims=True)).astype(jnp.bfloat16)
    attended = jnp.einsum("cqk,ckd->cqd", weights, value_rows, preferred_element_type=jnp.float32)
    return attended.astype(jnp.bfloat16)


def owner_layout(received, column, slot_count):
    source_count = column.shape[0]
    head_count = column.shape[1]
    upto_count = jnp.cumsum(column, axis=0)
    before_count = upto_count - column
    bucket_total = upto_count[-1]
    slot_range = jnp.arange(slot_count)
    source_dev = jnp.sum(upto_count[:, :, None] <= slot_range[None, None, :], axis=0)
    source_dev = jnp.minimum(source_dev, source_count - 1)
    source_range = jnp.arange(source_count)
    source_start = jnp.sum(
        jnp.where(source_dev[None] == source_range[:, None, None], before_count[:, :, None], 0),
        axis=0,
    )
    entry_row = jnp.clip(slot_range[None, :] - source_start, 0, received.shape[2] - 1)
    head_range = jnp.arange(head_count)
    layout = received[source_dev, head_range[:, None], entry_row]
    live = slot_range[None, :] < bucket_total[:, None]
    layout = jnp.where(live[..., None], layout, jnp.zeros((), layout.dtype))
    return (layout, live, before_count, bucket_total)


def tail_live(bucket_total, block_rows):
    return bucket_total[:, None] - block_rows + jnp.arange(block_rows)[None, :] >= 0


def last_rows(layout, bucket_total, block_rows):
    rank_index = bucket_total[:, None] - block_rows + jnp.arange(block_rows)[None, :]
    head_range = jnp.arange(layout.shape[0])
    rows = layout[head_range[:, None], jnp.maximum(rank_index, 0)]
    return jnp.where((rank_index >= 0)[..., None], rows, jnp.zeros((), rows.dtype))


def local(shared_qk, values, buckets, counts, w_out):
    tok_rows = shared_qk.shape[0]
    head_count = buckets.shape[1]
    head_dim = shared_qk.shape[1] // head_count
    seq_count = lax.axis_size("seq")
    capacity = 2 * tok_rows // seq_count
    slot_count = seq_count * capacity
    block_rows = BLOCK
    block_count = slot_count // block_rows
    own_index = lax.axis_index("seq")
    prev_index = (own_index + seq_count - 1) % seq_count
    head_range = jnp.arange(head_count)
    bucket_heads = buckets.T
    positions = jnp.arange(tok_rows)
    earlier = positions[None, :] < positions[:, None]
    same_bucket = bucket_heads[:, :, None] == bucket_heads[:, None, :]
    within = jnp.sum(same_bucket & earlier[None], axis=2)
    own_counts = lax.dynamic_index_in_dim(counts, own_index, 0, keepdims=False)
    own_starts = jnp.cumsum(own_counts, axis=1) - own_counts
    bucket_range = jnp.arange(seq_count)
    one_hot = bucket_heads[:, :, None] == bucket_range[None, None, :]
    token_start = jnp.sum(jnp.where(one_hot, own_starts[:, None, :], 0), axis=2)
    sorted_pos = token_start + within
    token_order = jnp.sum(
        jnp.where(sorted_pos[:, :, None] == positions[None, None, :], positions[None, :, None], 0),
        axis=1,
    )
    slot_range = jnp.arange(capacity)
    send_index = own_starts.T[:, :, None] + slot_range[None, None, :]
    filled = slot_range[None, None, :] < own_counts.T[:, :, None]
    token_pick = token_order[head_range[None, :, None], jnp.minimum(send_index, tok_rows - 1)]
    packed = jnp.concatenate(
        [
            shared_qk.reshape(tok_rows, head_count, head_dim),
            values.reshape(tok_rows, head_count, head_dim),
        ],
        axis=2,
    )
    outgoing = packed[token_pick, head_range[None, :, None]]
    outgoing = jnp.where(filled[..., None], outgoing, jnp.zeros((), outgoing.dtype))
    own_column = lax.dynamic_index_in_dim(counts, own_index, 2, keepdims=False)
    prev_column = lax.dynamic_index_in_dim(counts, prev_index, 2, keepdims=False)
    prev_total = jnp.sum(prev_column, axis=0)
    received = lax.all_to_all(outgoing, "seq", split_axis=0, concat_axis=0, tiled=True)
    layout, live, before_count, bucket_total = owner_layout(received, own_column, slot_count)
    tail_rows = last_rows(layout, bucket_total, block_rows)
    prev_rows = passed_along(tail_rows, "seq", 1)
    prev_live = tail_live(prev_total, block_rows)
    keys_all = jnp.concatenate([prev_rows, layout], axis=1)
    live_all = jnp.concatenate([prev_live, live], axis=1)
    window = jnp.concatenate(
        [
            keys_all[:, :slot_count].reshape(head_count, block_count, block_rows, 2 * head_dim),
            keys_all[:, block_rows:].reshape(head_count, block_count, block_rows, 2 * head_dim),
        ],
        axis=2,
    )
    window_live = jnp.concatenate(
        [
            live_all[:, :slot_count].reshape(head_count, block_count, block_rows),
            live_all[:, block_rows:].reshape(head_count, block_count, block_rows),
        ],
        axis=2,
    )
    queries = layout[..., :head_dim].reshape(head_count, block_count, block_rows, head_dim)
    attended = lax.map(
        lambda per_head: block_attention(per_head[0], per_head[1], per_head[2]),
        (queries, window, window_live),
    )
    out_layout = attended.reshape(head_count, slot_count, head_dim)
    back_index = before_count[:, :, None] + slot_range[None, None, :]
    back_filled = slot_range[None, None, :] < own_column[:, :, None]
    back_rows = out_layout[head_range[None, :, None], jnp.minimum(back_index, slot_count - 1)]
    back_rows = jnp.where(back_filled[..., None], back_rows, jnp.zeros((), back_rows.dtype))
    returned = lax.all_to_all(back_rows, "seq", split_axis=0, concat_axis=0, tiled=True)
    token_out = returned[buckets, head_range[None, :], within.T]
    token_out = token_out.reshape(tok_rows, head_count * head_dim)
    partial_sum = jnp.dot(token_out, w_out, preferred_element_type=jnp.float32)
    projected = lax.psum_scatter(partial_sum, "mp", scatter_dimension=1, tiled=True)
    return projected.astype(jnp.bfloat16)


def solution(mesh):
    placed = (P("seq", "mp"), P("seq", "mp"), P("seq", "mp"), P(None, "mp", None), P("mp", None))
    return jax.shard_map(
        local, mesh=mesh, in_specs=placed, out_specs=P("seq", "mp"), check_vma=False
    )
```

profile of v0, /device:TPU:0, one launch (start us, length us, event | category | flops | bytes accessed | tf_op | source)
XLA Modules:
  0.0 400.5 jit_solution(6937091656879628295)
XLA Ops:
  6.6 0.7 dynamic-slice_bitcast_fusion.1
  7.4 0.8 select_reduce_fusion.3
  8.3 1.4 convert_reduce_fusion
  10.4 25.6 %gather_fusion = s32[4096]{0:T(1024)S(1)} fusion(s32[16,128]{1,0:T(8,128)S(1)} %select_reduce_fusion.1, s32[4096]{0:T(1024)S(1)} %reshape.373), kind=kCustom, calls=%fused_computation | custom fusion | bytes 65536 | tf_op jit(solution)/shard_map/gather | solution.py:99
  36.8 21.6 %gather_fusion.1 = bf16[4096,256]{1,0:T(8,128)(2,1)S(1)} fusion(bf16[128,16,256]{2,1,0:T(8,128)(2,1)S(1)} %pad_maximum_fusion, s32[4096]{0:T(1024)S(1)} %reshape.379), kind=kCustom, calls=%fused_computation.1 | custom fusion | bytes 4227072 | tf_op jit(solution)/shard_map/gather | solution.py:107
  58.4 1.7 broadcast_select_fusion.2
  60.1 7.5 %all-to-all-start = ((bf16[16,16,16,256]{3,2,1,0:T(8,128)(2,1)}), bf16[16,16,16,256]{3,2,1,0:T(8,128)(2,1)S(1)}, u32[]{:S(2)}, u32[]{:S(2)}) async-start(bf16[16,16,16,256]{3,2,1,0:T(8,128)(2,1)} %broadcast_select_fusion.2), calls=%async_computation | async-start | bytes 4194304 | tf_op jit(solution)/shard_map/all_to_all | solution.py:112
  68.7 40.0 %all-to-all-done = bf16[16,16,16,256]{3,2,1,0:T(8,128)(2,1)S(1)} async-done(((bf16[16,16,16,256]{3,2,1,0:T(8,128)(2,1)}), bf16[16,16,16,256]{3,2,1,0:T(8,128)(2,1)S(1)}, u32[]{:S(2)}, u32[]{:S(2)}) %all-to-all-start) | async-done | bytes 2097184 | tf_op jit(solution)/shard_map/all_to_all | solution.py:112
  108.7 45.3 %gather_fusion.2 = bf16[4096,256]{1,0:T(8,128)(2,1)} fusion(bf16[16,16,16,256]{3,2,1,0:T(8,128)(2,1)S(1)} %all-to-all-done, s32[4096]{0:T(1024)S(1)} %bitcast.112), kind=kCustom, calls=%fused_computation.2 | custom fusion | bytes 4243456 | tf_op jit(solution)/shard_map/gather | solution.py:52
  154.0 1.9 broadcast_select_fusion.3
  155.9 40.7 %gather_fusion.3 = bf16[4096,256]{1,0:T(8,128)(2,1)} fusion(bf16[16,256,256]{2,1,0:T(8,128)(2,1)S(1)} %broadcast_select_fusion.3, s32[4096]{0:T(1024)S(1)} %bitcast.113), kind=kCustom, calls=%fused_computation.3 | custom fusion | bytes 4227072 | tf_op jit(solution)/shard_map/gather | solution.py:65
  196.6 2.9 broadcast_select_fusion.1
  199.5 1.0 collective-permute-start
  201.0 1.2 slice_bitcast_fusion.4
  202.2 0.6 copy-done
  202.7 0.8 broadcast_select_fusion
  203.6 29.9 %collective-permute-done = bf16[16,256,256]{2,1,0:T(8,128)(2,1)} collective-permute-done((bf16[16,256,256]{2,1,0:T(8,128)(2,1)}, bf16[16,256,256]{2,1,0:T(8,128)(2,1)}, u32[]{:S(2)}, u32[]{:S(2)}) %collective-permute-start) | collective-permute-done | bytes 2097184 | tf_op jit(solution)/shard_map/ppermute | solution.py:13
  233.4 3.9 maximum_bitcast_fusion
  237.3 47.1 %while.10 = (s32[]{:T(128)}, bf16[16,1,256,128]{3,2,1,0:T(8,128)(2,1)S(1)}, pred[16,1,512]{2,0,1:T(8,128)(4,1)S(1)}, bf16[16,1,256,128]{3,2,1,0:T(8,128)(2,1)}, bf16[16,1,512,256]{3,2,1,0:T(8,128)(2,1)}, /*index=5*/s32[]{:T(128)}) while((s32[]{:T(128)}, bf16[16,1,256,128]{3,2,1,0:T(8,128)(2,1)S(1)}, pred[16,1,512]{2,0,1:T(8,128)(4,1)S(1)}, ...), condition=%wide.region_11.12_spmd, body=%wide.region_8.11_spmd.sunk | while | flops 69369600 | bytes 2502737 | solution.py:134
  237.3 1.0 dynamic-slice_bitcast_fusion.4
  238.3 1.2 select_reduce_fusion.5
  239.8 0.4 fusion.47
  240.3 1.0 dynamic-slice_bitcast_fusion.4
  241.3 1.2 select_reduce_fusion.5
  243.2 1.0 dynamic-slice_bitcast_fusion.4
  244.2 1.2 select_reduce_fusion.5
  245.7 0.4 fusion.47
  246.2 1.0 dynamic-slice_bitcast_fusion.4
  247.1 1.2 select_reduce_fusion.5
  249.1 1.0 dynamic-slice_bitcast_fusion.4
  250.1 1.2 select_reduce_fusion.5
  251.6 0.4 fusion.47
  252.1 1.0 dynamic-slice_bitcast_fusion.4
  253.0 1.2 select_reduce_fusion.5
  255.0 1.0 dynamic-slice_bitcast_fusion.4
  256.0 1.2 select_reduce_fusion.5
  257.5 0.4 fusion.47
  258.0 1.0 dynamic-slice_bitcast_fusion.4
  258.9 1.2 select_reduce_fusion.5
  260.9 1.0 dynamic-slice_bitcast_fusion.4
  261.9 1.2 select_reduce_fusion.5
  263.4 0.4 fusion.47
  263.8 1.0 dynamic-slice_bitcast_fusion.4
  264.8 1.2 select_reduce_fusion.5
  266.8 1.0 dynamic-slice_bitcast_fusion.4
  267.8 1.2 select_reduce_fusion.5
  269.7 1.0 dynamic-slice_bitcast_fusion.4
  270.7 1.2 select_reduce_fusion.5
  272.7 1.0 dynamic-slice_bitcast_fusion.4
  273.7 1.2 select_reduce_fusion.5
  275.6 1.0 dynamic-slice_bitcast_fusion.4
  276.6 1.2 select_reduce_fusion.5
  278.6 1.0 dynamic-slice_bitcast_fusion.4
  279.6 1.2 select_reduce_fusion.5
  281.5 1.0 dynamic-slice_bitcast_fusion.4
  282.5 1.2 select_reduce_fusion.5
  284.4 21.7 %gather_fusion.4 = bf16[4096,128]{1,0:T(8,128)(2,1)S(1)} fusion(bf16[16,256,128]{2,1,0:T(8,128)(2,1)S(1)} %bitcast.114, s32[4096]{0:T(1024)S(1)} %reshape.397), kind=kCustom, calls=%fused_computation.4 | custom fusion | bytes 2129920 | tf_op jit(solution)/shard_map/gather | solution.py:141
  306.2 1.5 broadcast_select_fusion.4
  307.7 3.7 all-to-all-start.1
  311.8 22.4 %all-to-all-done.1 = bf16[16,16,16,128]{3,2,1,0:T(8,128)(2,1)S(1)} async-done(((bf16[16,16,16,128]{3,2,1,0:T(8,128)(2,1)}), bf16[16,16,16,128]{3,2,1,0:T(8,128)(2,1)S(1)}, u32[]{:S(2)}, u32[]{:S(2)}) %all-to-all-start.1) | async-done | bytes 1048608 | tf_op jit(solution)/shard_map/all_to_all | solution.py:143
  334.2 13.4 %gather_fusion.5 = bf16[2048,128]{1,0:T(8,128)(2,1)S(1)} fusion(bf16[16,16,16,128]{3,2,1,0:T(8,128)(2,1)S(1)} %all-to-all-done.1, s32[2048]{0:T(1024)S(1)} %reshape.403), kind=kCustom, calls=%fused_computation.5 | custom fusion | bytes 1073152 | tf_op jit(solution)/shard_map/gather | solution.py:144
  347.8 9.5 %fusion.41 = f32[128,4096]{1,0:T(8,128)} fusion(bf16[128,2048]{1,0:T(8,128)(2,1)S(1)} %reshape.372, bf16[2048,4096]{1,0:T(8,128)(2,1)} %param.11), kind=kOutput, calls=%fused_computation.103 | convolution fusion | flops 2147483648 | bytes 19398656 | tf_op jit(solution)/shard_map/dot_general | solution.py:146
  357.3 34.2 %reduce-scatter.2.cloned.1.call-done = f32[128,2048]{1,0:T(8,128)} async-done(((f32[128,4096]{1,0:T(8,128)}), f32[128,2048]{1,0:T(8,128)}) %reduce-scatter.2.cloned.1.call-update) | async-done | bytes 1048592 | tf_op jit(solution)/shard_map/reduce_scatter | solution.py:147
  391.5 2.1 convert_element_type.19
  (112 shorter events, 13.5 us)
Async XLA Ops:
  10.3 25.9 %copy-start.2 = (bf16[128,2048]{1,0:T(8,128)(2,1)S(1)}, bf16[128,2048]{1,0:T(8,128)(2,1)}, u32[]{:S(2)}) copy-start(bf16[128,2048]{1,0:T(8,128)(2,1)} %param.7) | copy-start | bytes 1572868
  10.3 26.0 %copy-start.3 = (bf16[128,2048]{1,0:T(8,128)(2,1)S(1)}, bf16[128,2048]{1,0:T(8,128)(2,1)}, u32[]{:S(2)}) copy-start(bf16[128,2048]{1,0:T(8,128)(2,1)} %param.8) | copy-start | bytes 1572868
  60.1 7.6 %copy-start.1 = (s32[16,16,16]{2,1,0:T(8,128)S(1)}, s32[16,16,16]{2,1,0:T(8,128)}, u32[]{:S(2)}) copy-start(s32[16,16,16]{2,1,0:T(8,128)} %param.10) | copy-start | bytes 49156
  60.1 48.5 %all-to-all-start = ((bf16[16,16,16,256]{3,2,1,0:T(8,128)(2,1)}), bf16[16,16,16,256]{3,2,1,0:T(8,128)(2,1)S(1)}, u32[]{:S(2)}, u32[]{:S(2)}) async-start(bf16[16,16,16,256]{3,2,1,0:T(8,128)(2,1)} %broadcast_select_fusion.2), calls=%async_computation | async-start | bytes 4194304 | tf_op jit(solution)/shard_map/all_to_all | solution.py:112
  199.5 33.9 %collective-permute-start = (bf16[16,256,256]{2,1,0:T(8,128)(2,1)}, bf16[16,256,256]{2,1,0:T(8,128)(2,1)}, u32[]{:S(2)}, u32[]{:S(2)}) collective-permute-start(bf16[16,256,256]{2,1,0:T(8,128)(2,1)} %broadcast_select_fusion.1), channel_id=1, source_target_pairs={{0,2},{2,4},{4,6},{6,8},{8,10},{10,12},{12,14},{14,16},{16,18},{18... | collective-permute-start | bytes 6291464 | tf_op jit(solution)/shard_map/ppermute | solution.py:13
  200.7 2.0 copy-start
  306.2 5.4 %copy-start.4 = (s32[128,16]{0,1:T(8,128)S(1)}, s32[128,16]{0,1:T(8,128)}, u32[]{:S(2)}) copy-start(s32[128,16]{0,1:T(8,128)} %param.9) | copy-start | bytes 24580
  307.7 26.5 %all-to-all-start.1 = ((bf16[16,16,16,128]{3,2,1,0:T(8,128)(2,1)}), bf16[16,16,16,128]{3,2,1,0:T(8,128)(2,1)S(1)}, u32[]{:S(2)}, u32[]{:S(2)}) async-start(bf16[16,16,16,128]{3,2,1,0:T(8,128)(2,1)} %broadcast_select_fusion.4), calls=%async_computation.1 | async-start | bytes 2097152 | tf_op jit(solution)/shard_map/all_to_all | solution.py:143
  311.4 80.2 %reduce-scatter.2.cloned.1.call-start = ((), (), s32[]{:S(2)}) async-start(), calls=%async_computation.3 | async-start | bytes 3145728 | tf_op jit(solution)/shard_map/reduce_scatter | solution.py:147
Sparse Core Ops, SparseCore 0:
  357.5 34.0 reduce-scatter.1
where the time goes:
time: 402 us; the launch traced here: 400 us
  local copies, waits for them, and re-layouts  188 us (47%)
  waiting for transfers between devices  126 us (31%)
  matrix products  35 us (9%)
  other arithmetic  24.3 us (6%)
  between operations  13.8 us (3%)
  starting transfers between devices  12.4 us (3%)
    gather x1, local copies, waits for them, and re-layouts, owner_layout(): layout = received[source_dev, head_range[:, None], entry_row]  45.3 us
    gather x1, local copies, waits for them, and re-layouts, last_rows(): rows = layout[head_range[:, None], jnp.maximum(rank_index, 0)]  40.7 us
    all_to_all x1, waiting for transfers between devices, local(): lax.all_to_all(outgoing, 'seq', split_axis=0, concat_axis=0, tiled=True)  40 us
    reduce_scatter x1, waiting for transfers between devices, local(): lax.psum_scatter(partial_sum, 'mp', scatter_dimension=1, tiled=True)  34.2 us
    ppermute x1, waiting for transfers between devices, passed_along(): lax.ppermute(shard, axis, [(i, (i + by) % devices) for i in range(devices)])  29.9 us
    gather x2, local copies, waits for them, and re-layouts, local(): token_order[head_range[None, :, None], jnp.minimum(send_index, tok_rows -...  25.7 us
    all_to_all x1, waiting for transfers between devices, local(): lax.all_to_all(back_rows, 'seq', split_axis=0, concat_axis=0, tiled=True)  22.4 us
    gather x1, local copies, waits for them, and re-layouts, local(): out_layout[head_range[None, :, None], jnp.minimum(back_index, slot_count...  21.7 us
  transfers between devices with their start and end apart: 4, of which 4 were waited for; matrix products, arithmetic and copies ran while one was open for 1% of the time, Pallas kernels for 0%

commit v1 on v0

--- a/solution.py
+++ b/solution.py
@@ -6,6 +6,21 @@
 
 BLOCK = 256
 SELF_SCORE = -100000.0
+
+
+def detail_spots(incoming_x, pos_dim, s0):
+    piece_now, long_array = (incoming_x.shape[:pos_dim], incoming_x.shape[pos_dim + 1 :])
+    return jnp.moveaxis(incoming_x.reshape(*piece_now, s0, -1, *long_array), pos_dim, 0)
+
+
+def _process_hubs(piece_in, along_dim):
+    piece_in = jnp.moveaxis(piece_in, 0, along_dim)
+    step_out = piece_in.shape
+    return piece_in.reshape(
+        *step_out[:along_dim],
+        step_out[along_dim] * step_out[along_dim + 1],
+        *step_out[along_dim + 2 :]
+    )
 
 
 def passed_along(shard, axis, by):
@@ -67,6 +82,21 @@
 
 
 def local(shared_qk, values, buckets, counts, w_out):
+
+    def stops_all_check(obj, across, block_here, q_in):
+        after, frame_out = (lax.axis_size(across), lax.axis_index(across))
+        current_arr = detail_spots(obj, block_here, after)
+        runs = [current_arr[frame_out]]
+        for t in [*range(1, after)]:
+            fresh = current_arr[(frame_out + t) % after]
+            runs.append(
+                lax.ppermute(
+                    fresh, axis_name=across, perm=[(q, (q + t) % after) for q in range(after)]
+                )
+            )
+        current_arr = jnp.stack(runs)[(frame_out - jnp.arange(after)) % after]
+        return _process_hubs(current_arr, q_in)
+
     tok_rows = shared_qk.shape[0]
     head_count = buckets.shape[1]
     head_dim = shared_qk.shape[1] // head_count
@@ -140,7 +170,7 @@
     back_filled = slot_range[None, None, :] < own_column[:, :, None]
     back_rows = out_layout[head_range[None, :, None], jnp.minimum(back_index, slot_count - 1)]
     back_rows = jnp.where(back_filled[..., None], back_rows, jnp.zeros((), back_rows.dtype))
-    returned = lax.all_to_all(back_rows, "seq", split_axis=0, concat_axis=0, tiled=True)
+    returned = stops_all_check(back_rows, "seq", 0, 0)
     token_out = returned[buckets, head_range[None, :], within.T]
     token_out = token_out.reshape(tok_rows, head_count * head_dim)
     partial_sum = jnp.dot(token_out, w_out, preferred_element_type=jnp.float32)

time: 402 us -> 426 us (1.060)
  local copies, waits for them, and re-layouts: 188 us -> 208 us
  starting transfers between devices: 12.4 us -> 25.5 us
  waiting for transfers between devices: 126 us -> 116 us
    all_to_all x1 -> x0, waiting for transfers between devices: 22.4 us -> none  [local(): lax.all_to_all(back_rows, 'seq', split_axis=0, concat_axis=0, tiled=True)]
    gather x1, local copies, waits for them, and re-layouts: 21.6 us -> 40.7 us  [local(): outgoing = packed[token_pick, head_range[None, :, None]]]
    ppermute x0 -> x15, starting transfers between devices: none -> 17 us  [stops_all_check(): lax.ppermute(fresh, axis_name=across, perm=[(q, (q + t) % after) for q in...]
    ppermute x0 -> x15, waiting for transfers between devices: none -> 12.8 us  [stops_all_check(): lax.ppermute(fresh, axis_name=across, perm=[(q, (q + t) % after) for q in...]
  transfers between devices with their start and end apart: 4 -> 18, of which waited for: 4 -> 9; matrix products, arithmetic and copies ran while one was open for 1% -> 1% of each run, Pallas kernels for 0% -> 0%
where the time goes in v1:
time: 426 us; the launch traced here: 424 us
  local copies, waits for them, and re-layouts  208 us (49%)
  waiting for transfers between devices  116 us (27%)
  matrix products  35 us (8%)
  starting transfers between devices  25.5 us (6%)
  other arithmetic  24.7 us (6%)
  between operations  13.9 us (3%)
    gather x1, local copies, waits for them, and re-layouts, owner_layout(): layout = received[source_dev, head_range[:, None], entry_row]  45.3 us
    gather x1, local copies, waits for them, and re-layouts, local(): outgoing = packed[token_pick, head_range[None, :, None]]  40.7 us
    gather x1, local copies, waits for them, and re-layouts, last_rows(): rows = layout[head_range[:, None], jnp.maximum(rank_index, 0)]  40.7 us
    all_to_all x1, waiting for transfers between devices, local(): lax.all_to_all(outgoing, 'seq', split_axis=0, concat_axis=0, tiled=True)  39.9 us
    reduce_scatter x1, waiting for transfers between devices, local(): lax.psum_scatter(partial_sum, 'mp', scatter_dimension=1, tiled=True)  33.4 us
    ppermute x1, waiting for transfers between devices, passed_along(): lax.ppermute(shard, axis, [(i, (i + by) % devices) for i in range(devices)])  29.6 us
    gather x2, local copies, waits for them, and re-layouts, local(): token_order[head_range[None, :, None], jnp.minimum(send_index, tok_rows -...  25.7 us
    gather x1, local copies, waits for them, and re-layouts, local(): out_layout[head_range[None, :, None], jnp.minimum(back_index, slot_count...  21.7 us
  transfers between devices with their start and end apart: 18, of which 9 were waited for; matrix products, arithmetic and copies ran while one was open for 1% of the time, Pallas kernels for 0%

profile of v1, /device:TPU:0, one launch (start us, length us, event | category | flops | bytes accessed | tf_op | source)
XLA Modules:
  0.0 423.7 jit_solution(9318320866908785657)
XLA Ops:
  8.3 1.4 convert_reduce_fusion
  10.4 25.6 %gather_fusion = s32[4096]{0:T(1024)S(1)} fusion(s32[16,128]{1,0:T(8,128)S(1)} %select_reduce_fusion.1, s32[4096]{0:T(1024)S(1)} %reshape.458), kind=kCustom, calls=%fused_computation | custom fusion | bytes 65536 | tf_op jit(solution)/shard_map/gather | solution.py:129
  36.8 40.7 %gather_fusion.1 = bf16[4096,256]{1,0:T(8,128)(2,1)} fusion(bf16[128,16,256]{2,1,0:T(8,128)(2,1)S(1)} %pad_maximum_fusion, s32[4096]{0:T(1024)S(1)} %reshape.464), kind=kCustom, calls=%fused_computation.1 | custom fusion | bytes 4227072 | tf_op jit(solution)/shard_map/gather | solution.py:137
  77.5 2.9 broadcast_select_fusion.2
  80.4 7.5 %all-to-all-start = ((bf16[16,16,16,256]{3,2,1,0:T(8,128)(2,1)}), bf16[16,16,16,256]{3,2,1,0:T(8,128)(2,1)S(1)}, u32[]{:S(2)}, u32[]{:S(2)}) async-start(bf16[16,16,16,256]{3,2,1,0:T(8,128)(2,1)} %broadcast_select_fusion.2), calls=%async_computation | async-start | bytes 4194304 | tf_op jit(solution)/shard_map/all_to_all | solution.py:142
  89.0 39.9 %all-to-all-done = bf16[16,16,16,256]{3,2,1,0:T(8,128)(2,1)S(1)} async-done(((bf16[16,16,16,256]{3,2,1,0:T(8,128)(2,1)}), bf16[16,16,16,256]{3,2,1,0:T(8,128)(2,1)S(1)}, u32[]{:S(2)}, u32[]{:S(2)}) %all-to-all-start) | async-done | bytes 2097184 | tf_op jit(solution)/shard_map/all_to_all | solution.py:142
  128.9 45.3 %gather_fusion.2 = bf16[4096,256]{1,0:T(8,128)(2,1)} fusion(bf16[16,16,16,256]{3,2,1,0:T(8,128)(2,1)S(1)} %all-to-all-done, s32[4096]{0:T(1024)S(1)} %bitcast.147), kind=kCustom, calls=%fused_computation.2 | custom fusion | bytes 4243456 | tf_op jit(solution)/shard_map/gather | solution.py:67
  174.3 1.9 broadcast_select_fusion.3
  176.2 40.7 %gather_fusion.3 = bf16[4096,256]{1,0:T(8,128)(2,1)} fusion(bf16[16,256,256]{2,1,0:T(8,128)(2,1)S(1)} %broadcast_select_fusion.3, s32[4096]{0:T(1024)S(1)} %bitcast.148), kind=kCustom, calls=%fused_computation.3 | custom fusion | bytes 4227072 | tf_op jit(solution)/shard_map/gather | solution.py:80
  216.9 2.9 broadcast_select_fusion.1
  219.8 1.0 collective-permute-start
  221.5 1.2 slice_bitcast_fusion.4
  223.2 0.8 broadcast_select_fusion
  224.1 29.6 %collective-permute-done = bf16[16,256,256]{2,1,0:T(8,128)(2,1)} collective-permute-done((bf16[16,256,256]{2,1,0:T(8,128)(2,1)}, bf16[16,256,256]{2,1,0:T(8,128)(2,1)}, u32[]{:S(2)}, u32[]{:S(2)}) %collective-permute-start) | collective-permute-done | bytes 2097184 | tf_op jit(solution)/shard_map/ppermute | solution.py:28
  253.7 3.9 maximum_bitcast_fusion
  257.6 47.1 %while.10 = (s32[]{:T(128)}, bf16[16,1,256,128]{3,2,1,0:T(8,128)(2,1)S(1)}, pred[16,1,512]{2,0,1:T(8,128)(4,1)S(1)}, bf16[16,1,256,128]{3,2,1,0:T(8,128)(2,1)}, bf16[16,1,512,256]{3,2,1,0:T(8,128)(2,1)}, /*index=5*/s32[]{:T(128)}) while((s32[]{:T(128)}, bf16[16,1,256,128]{3,2,1,0:T(8,128)(2,1)S(1)}, pred[16,1,512]{2,0,1:T(8,128)(4,1)S(1)}, ...), condition=%wide.region_11.12_spmd, body=%wide.region_8.11_spmd.sunk | while | flops 69369600 | bytes 2502737 | solution.py:164
  257.6 1.0 dynamic-slice_bitcast_fusion.4
  258.6 1.2 select_reduce_fusion.5
  260.6 1.0 dynamic-slice_bitcast_fusion.4
  261.5 1.2 select_reduce_fusion.5
  263.5 1.0 dynamic-slice_bitcast_fusion.4
  264.5 1.2 select_reduce_fusion.5
  266.5 1.0 dynamic-slice_bitcast_fusion.4
  267.4 1.2 select_reduce_fusion.5
  269.4 1.0 dynamic-slice_bitcast_fusion.4
  270.4 1.2 select_reduce_fusion.5
  272.3 1.0 dynamic-slice_bitcast_fusion.4
  273.3 1.2 select_reduce_fusion.5
  275.3 1.0 dynamic-slice_bitcast_fusion.4
  276.3 1.2 select_reduce_fusion.5
  278.2 1.0 dynamic-slice_bitcast_fusion.4
  279.2 1.2 select_reduce_fusion.5
  281.2 1.0 dynamic-slice_bitcast_fusion.4
  282.2 1.2 select_reduce_fusion.5
  284.1 1.0 dynamic-slice_bitcast_fusion.4
  285.1 1.2 select_reduce_fusion.5
  287.1 1.0 dynamic-slice_bitcast_fusion.4
  288.1 1.2 select_reduce_fusion.5
  290.0 1.0 dynamic-slice_bitcast_fusion.4
  291.0 1.2 select_reduce_fusion.5
  293.0 1.0 dynamic-slice_bitcast_fusion.4
  294.0 1.2 select_reduce_fusion.5
  295.9 1.0 dynamic-slice_bitcast_fusion.4
  296.9 1.2 select_reduce_fusion.5
  298.9 1.0 dynamic-slice_bitcast_fusion.4
  299.9 1.2 select_reduce_fusion.5
  301.8 1.0 dynamic-slice_bitcast_fusion.4
  302.8 1.2 select_reduce_fusion.5
  304.7 21.7 %gather_fusion.4 = bf16[4096,128]{1,0:T(8,128)(2,1)S(1)} fusion(bf16[16,256,128]{2,1,0:T(8,128)(2,1)S(1)} %bitcast.149, s32[4096]{0:T(1024)S(1)} %reshape.482), kind=kCustom, calls=%fused_computation.4 | custom fusion | bytes 2129920 | tf_op jit(solution)/shard_map/gather | solution.py:171
  327.6 2.3 collective-permute-start.3
  329.9 1.7 collective-permute-start.4
  331.5 2.4 collective-permute-done.1
  334.3 0.9 collective-permute-done.2
  335.2 1.8 collective-permute-start.7
  337.8 1.4 collective-permute-start.9
  339.2 6.5 %collective-permute-done.5 = bf16[1,16,16,128]{3,2,1,0:T(8,128)(2,1)S(1)} collective-permute-done((bf16[1,16,16,128]{3,2,1,0:T(8,128)(2,1)S(1)}, bf16[1,16,16,128]{3,2,1,0:T(8,128)(2,1)S(1)}, u32[]{:S(2)}, u32[]{:S(2)}) %collective-permute-start.5) | collective-permute-done | bytes 65568 | tf_op jit(solution)/shard_map/ppermute | solution.py:93
  346.4 3.7 collective-permute-start.12
  350.2 0.8 collective-permute-start.13
  351.0 3.3 collective-permute-start.14
  354.7 2.1 collective-permute-done.14
  358.3 13.4 %gather_fusion.6 = bf16[2048,128]{1,0:T(8,128)(2,1)S(1)} fusion(bf16[16,16,16,128]{3,2,1,0:T(8,128)(2,1)S(1)} %gather_fusion.5, s32[2048]{0:T(1024)S(1)} %reshape.498), kind=kCustom, calls=%fused_computation.6 | custom fusion | bytes 1073152 | tf_op jit(solution)/shard_map/gather | solution.py:174
  371.9 9.5 %fusion.43 = f32[128,4096]{1,0:T(8,128)} fusion(bf16[128,2048]{1,0:T(8,128)(2,1)S(1)} %reshape.457, bf16[2048,4096]{1,0:T(8,128)(2,1)} %param.11), kind=kOutput, calls=%fused_computation.142 | convolution fusion | flops 2147483648 | bytes 19398656 | tf_op jit(solution)/shard_map/dot_general | solution.py:176
  381.4 33.4 %reduce-scatter.2.cloned.1.call-done = f32[128,2048]{1,0:T(8,128)} async-done(((f32[128,4096]{1,0:T(8,128)}), f32[128,2048]{1,0:T(8,128)}) %reduce-scatter.2.cloned.1.call-update) | async-done | bytes 1048592 | tf_op jit(solution)/shard_map/reduce_scatter | solution.py:177
  414.8 2.1 convert_element_type.19
  (160 shorter events, 22.2 us)
Async XLA Ops:
  10.3 25.9 %copy-start.2 = (bf16[128,2048]{1,0:T(8,128)(2,1)S(1)}, bf16[128,2048]{1,0:T(8,128)(2,1)}, u32[]{:S(2)}) copy-start(bf16[128,2048]{1,0:T(8,128)(2,1)} %param.7) | copy-start | bytes 1572868
  10.3 26.0 %copy-start.3 = (bf16[128,2048]{1,0:T(8,128)(2,1)S(1)}, bf16[128,2048]{1,0:T(8,128)(2,1)}, u32[]{:S(2)}) copy-start(bf16[128,2048]{1,0:T(8,128)(2,1)} %param.8) | copy-start | bytes 1572868
  80.4 7.6 %copy-start.1 = (s32[16,16,16]{2,1,0:T(8,128)S(1)}, s32[16,16,16]{2,1,0:T(8,128)}, u32[]{:S(2)}) copy-start(s32[16,16,16]{2,1,0:T(8,128)} %param.10) | copy-start | bytes 49156
  80.4 48.5 %all-to-all-start = ((bf16[16,16,16,256]{3,2,1,0:T(8,128)(2,1)}), bf16[16,16,16,256]{3,2,1,0:T(8,128)(2,1)S(1)}, u32[]{:S(2)}, u32[]{:S(2)}) async-start(bf16[16,16,16,256]{3,2,1,0:T(8,128)(2,1)} %broadcast_select_fusion.2), calls=%async_computation | async-start | bytes 4194304 | tf_op jit(solution)/shard_map/all_to_all | solution.py:142
  88.0 326.8 %reduce-scatter.2.cloned.1.call-start = ((), (), s32[]{:S(2)}) async-start(), calls=%async_computation.2 | async-start | bytes 3145728 | tf_op jit(solution)/shard_map/reduce_scatter | solution.py:177
  216.9 4.1 copy-start.4
  219.8 33.9 %collective-permute-start = (bf16[16,256,256]{2,1,0:T(8,128)(2,1)}, bf16[16,256,256]{2,1,0:T(8,128)(2,1)}, u32[]{:S(2)}, u32[]{:S(2)}) collective-permute-start(bf16[16,256,256]{2,1,0:T(8,128)(2,1)} %broadcast_select_fusion.1), channel_id=1, source_target_pairs={{0,2},{2,4},{4,6},{6,8},{8,10},{10,12},{12,14},{14,16},{16,18},{18... | collective-permute-start | bytes 6291464 | tf_op jit(solution)/shard_map/ppermute | solution.py:28
  221.3 2.0 copy-start
  327.5 6.5 %collective-permute-start.1 = (bf16[1,16,16,128]{3,2,1,0:T(8,128)(2,1)S(1)}, bf16[1,16,16,128]{3,2,1,0:T(8,128)(2,1)S(1)}, u32[]{:S(2)}, u32[]{:S(2)}) collective-permute-start(bf16[1,16,16,128]{3,2,1,0:T(8,128)(2,1)S(1)} %get-tuple-element.79), channel_id=1, source_target_pairs={{0,2},{2,4},{4,6},{6,8},{8,10},{10,12},{12,14},{14,16},{16,18},{18... | collective-permute-start | bytes 196616 | tf_op jit(solution)/shard_map/ppermute | solution.py:93
  327.5 7.7 %collective-permute-start.2 = (bf16[1,16,16,128]{3,2,1,0:T(8,128)(2,1)S(1)}, bf16[1,16,16,128]{3,2,1,0:T(8,128)(2,1)S(1)}, u32[]{:S(2)}, u32[]{:S(2)}) collective-permute-start(bf16[1,16,16,128]{3,2,1,0:T(8,128)(2,1)S(1)} %get-tuple-element.78), channel_id=1, source_target_pairs={{0,4},{2,6},{4,8},{6,10},{8,12},{10,14},{12,16},{14,18},{16,20},{1... | collective-permute-start | bytes 196616 | tf_op jit(solution)/shard_map/ppermute | solution.py:93
  327.6 9.4 %collective-permute-start.3 = (bf16[1,16,16,128]{3,2,1,0:T(8,128)(2,1)S(1)}, bf16[1,16,16,128]{3,2,1,0:T(8,128)(2,1)S(1)}, u32[]{:S(2)}, u32[]{:S(2)}) collective-permute-start(bf16[1,16,16,128]{3,2,1,0:T(8,128)(2,1)S(1)} %get-tuple-element.77), channel_id=1, source_target_pairs={{0,6},{2,8},{4,10},{6,12},{8,14},{10,16},{12,18},{14,20},{16,22},{... | collective-permute-start | bytes 196616 | tf_op jit(solution)/shard_map/ppermute | solution.py:93
  329.9 7.9 %collective-permute-start.4 = (bf16[1,16,16,128]{3,2,1,0:T(8,128)(2,1)S(1)}, bf16[1,16,16,128]{3,2,1,0:T(8,128)(2,1)S(1)}, u32[]{:S(2)}, u32[]{:S(2)}) collective-permute-start(bf16[1,16,16,128]{3,2,1,0:T(8,128)(2,1)S(1)} %get-tuple-element.76), channel_id=1, source_target_pairs={{0,8},{2,10},{4,12},{6,14},{8,16},{10,18},{12,20},{14,22},{16,24},... | collective-permute-start | bytes 196616 | tf_op jit(solution)/shard_map/ppermute | solution.py:93
  331.5 14.2 %collective-permute-start.5 = (bf16[1,16,16,128]{3,2,1,0:T(8,128)(2,1)S(1)}, bf16[1,16,16,128]{3,2,1,0:T(8,128)(2,1)S(1)}, u32[]{:S(2)}, u32[]{:S(2)}) collective-permute-start(bf16[1,16,16,128]{3,2,1,0:T(8,128)(2,1)S(1)} %get-tuple-element.75), channel_id=1, source_target_pairs={{0,10},{2,12},{4,14},{6,16},{8,18},{10,20},{12,22},{14,24},{16,26}... | collective-permute-start | bytes 196616 | tf_op jit(solution)/shard_map/ppermute | solution.py:93
  334.0 12.0 %collective-permute-start.6 = (bf16[1,16,16,128]{3,2,1,0:T(8,128)(2,1)S(1)}, bf16[1,16,16,128]{3,2,1,0:T(8,128)(2,1)S(1)}, u32[]{:S(2)}, u32[]{:S(2)}) collective-permute-start(bf16[1,16,16,128]{3,2,1,0:T(8,128)(2,1)S(1)} %get-tuple-element.74), channel_id=1, source_target_pairs={{0,12},{2,14},{4,16},{6,18},{8,20},{10,22},{12,24},{14,26},{16,28}... | collective-permute-start | bytes 196616 | tf_op jit(solution)/shard_map/ppermute | solution.py:93
  335.2 11.2 %collective-permute-start.7 = (bf16[1,16,16,128]{3,2,1,0:T(8,128)(2,1)S(1)}, bf16[1,16,16,128]{3,2,1,0:T(8,128)(2,1)S(1)}, u32[]{:S(2)}, u32[]{:S(2)}) collective-permute-start(bf16[1,16,16,128]{3,2,1,0:T(8,128)(2,1)S(1)} %get-tuple-element.73), channel_id=1, source_target_pairs={{0,14},{2,16},{4,18},{6,20},{8,22},{10,24},{12,26},{14,28},{16,30}... | collective-permute-start | bytes 196616 | tf_op jit(solution)/shard_map/ppermute | solution.py:93
  337.0 13.2 %collective-permute-start.8 = (bf16[1,16,16,128]{3,2,1,0:T(8,128)(2,1)S(1)}, bf16[1,16,16,128]{3,2,1,0:T(8,128)(2,1)S(1)}, u32[]{:S(2)}, u32[]{:S(2)}) collective-permute-start(bf16[1,16,16,128]{3,2,1,0:T(8,128)(2,1)S(1)} %get-tuple-element.72), channel_id=1, source_target_pairs={{0,16},{2,18},{4,20},{6,22},{8,24},{10,26},{12,28},{14,30},{16,0},... | collective-permute-start | bytes 196616 | tf_op jit(solution)/shard_map/ppermute | solution.py:93
  337.8 13.3 %collective-permute-start.9 = (bf16[1,16,16,128]{3,2,1,0:T(8,128)(2,1)S(1)}, bf16[1,16,16,128]{3,2,1,0:T(8,128)(2,1)S(1)}, u32[]{:S(2)}, u32[]{:S(2)}) collective-permute-start(bf16[1,16,16,128]{3,2,1,0:T(8,128)(2,1)S(1)} %get-tuple-element.71), channel_id=1, source_target_pairs={{0,18},{2,20},{4,22},{6,24},{8,26},{10,28},{12,30},{14,0},{16,2},{... | collective-permute-start | bytes 196616 | tf_op jit(solution)/shard_map/ppermute | solution.py:93
  345.7 8.6 %collective-permute-start.10 = (bf16[1,16,16,128]{3,2,1,0:T(8,128)(2,1)S(1)}, bf16[1,16,16,128]{3,2,1,0:T(8,128)(2,1)S(1)}, u32[]{:S(2)}, u32[]{:S(2)}) collective-permute-start(bf16[1,16,16,128]{3,2,1,0:T(8,128)(2,1)S(1)} %get-tuple-element.70), channel_id=1, source_target_pairs={{0,20},{2,22},{4,24},{6,26},{8,28},{10,30},{12,0},{14,2},{16,4},{1... | collective-permute-start | bytes 196616 | tf_op jit(solution)/shard_map/ppermute | solution.py:93
  345.9 8.7 %collective-permute-start.11 = (bf16[1,16,16,128]{3,2,1,0:T(8,128)(2,1)S(1)}, bf16[1,16,16,128]{3,2,1,0:T(8,128)(2,1)S(1)}, u32[]{:S(2)}, u32[]{:S(2)}) collective-permute-start(bf16[1,16,16,128]{3,2,1,0:T(8,128)(2,1)S(1)} %get-tuple-element.69), channel_id=1, source_target_pairs={{0,22},{2,24},{4,26},{6,28},{8,30},{10,0},{12,2},{14,4},{16,6},{18... | collective-permute-start | bytes 196616 | tf_op jit(solution)/shard_map/ppermute | solution.py:93
  346.4 8.2 %collective-permute-start.12 = (bf16[1,16,16,128]{3,2,1,0:T(8,128)(2,1)S(1)}, bf16[1,16,16,128]{3,2,1,0:T(8,128)(2,1)S(1)}, u32[]{:S(2)}, u32[]{:S(2)}) collective-permute-start(bf16[1,16,16,128]{3,2,1,0:T(8,128)(2,1)S(1)} %get-tuple-element.68), channel_id=1, source_target_pairs={{0,24},{2,26},{4,28},{6,30},{8,0},{10,2},{12,4},{14,6},{16,8},{18,... | collective-permute-start | bytes 196616 | tf_op jit(solution)/shard_map/ppermute | solution.py:93
  350.2 4.5 %collective-permute-start.13 = (bf16[1,16,16,128]{3,2,1,0:T(8,128)(2,1)S(1)}, bf16[1,16,16,128]{3,2,1,0:T(8,128)(2,1)S(1)}, u32[]{:S(2)}, u32[]{:S(2)}) collective-permute-start(bf16[1,16,16,128]{3,2,1,0:T(8,128)(2,1)S(1)} %get-tuple-element.67), channel_id=1, source_target_pairs={{0,26},{2,28},{4,30},{6,0},{8,2},{10,4},{12,6},{14,8},{16,10},{18,... | collective-permute-start | bytes 196616 | tf_op jit(solution)/shard_map/ppermute | solution.py:93
  351.0 5.8 %collective-permute-start.14 = (bf16[1,16,16,128]{3,2,1,0:T(8,128)(2,1)S(1)}, bf16[1,16,16,128]{3,2,1,0:T(8,128)(2,1)S(1)}, u32[]{:S(2)}, u32[]{:S(2)}) collective-permute-start(bf16[1,16,16,128]{3,2,1,0:T(8,128)(2,1)S(1)} %get-tuple-element.66), channel_id=1, source_target_pairs={{0,28},{2,30},{4,0},{6,2},{8,4},{10,6},{12,8},{14,10},{16,12},{18,... | collective-permute-start | bytes 196616 | tf_op jit(solution)/shard_map/ppermute | solution.py:93
  354.3 3.2 collective-permute-start.15
Sparse Core Ops, SparseCore 0:
  381.5 33.2 reduce-scatter.1
